TPU v7x, 32 devices: a whole 2x2x4 slice. The times are simulated.
32 devices in a mesh: dp: 2 (over x), ctx: 16 (over z, y, core).
Axes of the slice: x: 2, y: 2, z: 4, core: 2. Of those that a mesh axis runs over, the one named last changes fastest.
Arguments:
- features: bfloat16 [2, 2048, 1536], P('dp', 'ctx'), may hold values from -500 to 500
- gain: float32 [1536], replicated, may hold values from 0.1 to 1.9
- conv_weight: bfloat16 [5, 1536, 768], replicated, may hold values from -0.0625 to 0.0625
- cotangent: bfloat16 [2, 2048, 768], P('dp', 'ctx'), may hold values from -15 to 15
Outputs:
- convolved: bfloat16 [2, 2048, 768], P('dp', 'ctx')
- input_grad: bfloat16 [2, 2048, 1536], P('dp', 'ctx')
- gain_grad: float32 [1536], replicated
All inputs are finite; a program needn't handle non-finite values.
Results may differ from a plain program's by a relative error of at most 0.0054.
Values may be sent and summed in bfloat16 or wider, within the bound.
A program may use at most 64 MiB of HBM per device.

v0:
```python
import math
import jax
import jax.numpy as jnp
from jax import lax
from jax.sharding import PartitionSpec as P

KERNEL_TAPS = 5
EPS = 1e-06


def shifted(block, axis, distance):
    devices = range(lax.axis_size(axis))
    route = [(i - distance, i) for i in devices if i - distance in devices]
    return lax.ppermute(block, axis, route)


def activate(values):
    return jax.nn.gelu(values, approximate=True)


def flip_channels(values):
    return values[:, :, ::-1]


def taps_ahead(values, shard_hops):
    pieces = []
    for tap_index in range(KERNEL_TAPS):
        if tap_index == KERNEL_TAPS // 2:
            pieces.append(values)
        else:
            pieces.append(shifted(values, "ctx", -(tap_index - KERNEL_TAPS // 2) * shard_hops))
    return pieces


def taps_behind(values, shard_hops):
    pieces = []
    for tap_index in range(KERNEL_TAPS):
        if tap_index == KERNEL_TAPS // 2:
            pieces.append(values)
        else:
            pieces.append(shifted(values, "ctx", (tap_index - KERNEL_TAPS // 2) * shard_hops))
    return pieces


def apply_forward(pieces, weight):
    lead = pieces[0].shape[0]
    middle = pieces[0].shape[1]
    total = jnp.zeros((lead * middle, weight.shape[2]), jnp.float32)
    for tap_index in range(KERNEL_TAPS):
        flat_rows = pieces[tap_index].reshape(lead * middle, pieces[tap_index].shape[2])
        total = total + jnp.dot(flat_rows, weight[tap_index], preferred_element_type=jnp.float32)
    return total.reshape(lead, middle, weight.shape[2])


def apply_backward(pieces, weight):
    lead = pieces[0].shape[0]
    middle = pieces[0].shape[1]
    total = jnp.zeros((lead * middle, weight.shape[1]), jnp.float32)
    for tap_index in range(KERNEL_TAPS):
        flat_rows = pieces[tap_index].reshape(lead * middle, pieces[tap_index].shape[2])
        total = total + lax.dot_general(
            flat_rows,
            weight[tap_index],
            (((1,), (1,)), ((), ())),
            preferred_element_type=jnp.float32,
        )
    return total.reshape(lead, middle, weight.shape[1])


def per_device(features, gain, conv_weight, cotangent):
    shard_hops = lax.axis_size("ctx") // 8
    wide = features.astype(jnp.float32)
    inv_rms = lax.rsqrt(jnp.mean(wide * wide, axis=-1, keepdims=True) + EPS)
    normed = wide * inv_rms
    scaled = normed * gain
    hidden = activate(scaled).astype(jnp.bfloat16)
    ahead = taps_ahead(hidden, shard_hops)
    forward_term = apply_forward(ahead, conv_weight)
    flipped = [
        flip_channels(ahead[KERNEL_TAPS - 1 - tap_index]) for tap_index in range(KERNEL_TAPS)
    ]
    reverse_term = flip_channels(apply_forward(flipped, conv_weight).astype(jnp.bfloat16))
    convolved = (forward_term + reverse_term.astype(jnp.float32)).astype(jnp.bfloat16)
    behind = taps_behind(cotangent, shard_hops)
    back_forward = apply_backward(behind, conv_weight)
    flipped_grads = [
        flip_channels(behind[KERNEL_TAPS - 1 - tap_index]) for tap_index in range(KERNEL_TAPS)
    ]
    back_reverse = flip_channels(apply_backward(flipped_grads, conv_weight).astype(jnp.bfloat16))
    grad_hidden = back_forward + back_reverse.astype(jnp.float32)
    _, pullback = jax.vjp(activate, scaled)
    grad_scaled = pullback(grad_hidden)[0]
    partial_sum = jnp.sum(grad_scaled * normed, axis=(0, 1))
    summed = lax.psum(partial_sum, ("dp", "ctx"))
    total_rows = features.shape[0] * features.shape[1] * lax.axis_size("dp") * lax.axis_size("ctx")
    gain_grad = summed / math.sqrt(total_rows)
    grad_normed = grad_scaled * gain
    spread_term = jnp.mean(grad_normed * normed, axis=-1, keepdims=True)
    input_grad = (inv_rms * (grad_normed - normed * spread_term)).astype(jnp.bfloat16)
    return (convolved, input_grad, gain_grad)


def solution(mesh):
    return jax.shard_map(
        per_device,
        mesh=mesh,
        in_specs=(P("dp", "ctx", None), P(), P(), P("dp", "ctx", None)),
        out_specs=(P("dp", "ctx", None), P("dp", "ctx", None), P()),
        check_vma=False,
    )
```

profile of v0, /device:TPU:0, one launch (start us, length us, event | category | flops | bytes accessed | tf_op | source)
XLA Modules:
  0.0 152.5 jit_solution(12865565920787407074)
XLA Ops:
  0.6 4.9 %collective-permute-start.6 = (bf16[1,128,768]{2,1,0:T(8,128)(2,1)}, bf16[1,128,768]{2,1,0:T(8,128)(2,1)S(1)}, u32[]{:S(2)}, u32[]{:S(2)}) collective-permute-start(bf16[1,128,768]{2,1,0:T(8,128)(2,1)} %param.7), channel_id=1, source_target_pairs={{0,2},{1,3},{2,4},{3,5},{4,6},{5,7},{6,8},{7,9},{8,10},{9,11},{10,... | collective-permute-start | bytes 589832 | tf_op jit(solution)/shard_map/ppermute | solution.py:14
  5.5 3.5 %collective-permute-start.7 = (bf16[1,128,768]{2,1,0:T(8,128)(2,1)}, bf16[1,128,768]{2,1,0:T(8,128)(2,1)S(1)}, u32[]{:S(2)}, u32[]{:S(2)}) collective-permute-start(bf16[1,128,768]{2,1,0:T(8,128)(2,1)} %param.7), channel_id=1, source_target_pairs={{0,4},{1,5},{2,6},{3,7},{4,8},{5,9},{6,10},{7,11},{8,12},{9,13},{1... | collective-permute-start | bytes 589832 | tf_op jit(solution)/shard_map/ppermute | solution.py:14
  11.6 2.7 %rev.39 = bf16[1,128,768]{2,1,0:T(8,128)(2,1)S(1)} reverse(bf16[1,128,768]{2,1,0:T(8,128)(2,1)} %param.7), dimensions={2} | reverse | bytes 393216 | tf_op jit(solution)/shard_map/rev | solution.py:22
  14.3 2.7 %fusion.23 = f32[128,1536]{1,0:T(8,128)S(1)} fusion(bf16[5,1536,768]{2,1,0:T(8,128)(2,1)} %param.6, bf16[1,128,768]{2,1,0:T(8,128)(2,1)} %param.7), kind=kOutput, calls=%fused_computation.27 | convolution fusion | flops 301989888 | bytes 3342336 | tf_op jit(solution)/shard_map/dot_general | solution.py:61
  17.0 2.6 %fusion.21 = f32[128,1536]{1,0:T(8,128)S(1)} fusion(bf16[5,1536,768]{2,1,0:T(8,128)(2,1)} %param.6, bf16[1,128,768]{2,1,0:T(8,128)(2,1)S(1)} %rev.39), kind=kOutput, calls=%fused_computation.25 | convolution fusion | flops 301989888 | bytes 3342336 | tf_op jit(solution)/shard_map/dot_general | solution.py:61
  21.4 2.5 %fusion.29 = f32[128,1536]{1,0:T(8,128)S(1)} fusion(bf16[5,1536,768]{2,1,0:T(8,128)(2,1)} %param.6, bf16[1,128,768]{2,1,0:T(8,128)(2,1)S(1)} %rev.38), kind=kOutput, calls=%fused_computation.33 | convolution fusion | flops 301989888 | bytes 3342336 | tf_op jit(solution)/shard_map/dot_general | solution.py:61
  26.8 2.7 %fusion.1 = f32[128,1536]{1,0:T(8,128)S(1)} fusion(f32[128,1536]{1,0:T(8,128)S(1)} %fusion.21, f32[128,1536]{1,0:T(8,128)S(1)} %fusion.29, bf16[5,1536,768]{2,1,0:T(8,128)(2,1)} %param.6, bf16[1,128,768]{2,1,0:T(8,128)(2,1)} %rev.37), kind=kOutput, calls=%fused_computation.3 | convolution fusion | flops 302383104 | bytes 4915200 | tf_op jit(solution)/shard_map/dot_general | solution.py:61
  29.6 2.7 %rev.41 = bf16[1,128,768]{2,1,0:T(8,128)(2,1)S(1)} reverse(bf16[1,128,768]{2,1,0:T(8,128)(2,1)} %collective-permute-done.4), dimensions={2} | reverse | bytes 393216 | tf_op jit(solution)/shard_map/rev | solution.py:22
  32.3 2.6 %fusion.7 = f32[128,1536]{1,0:T(8,128)S(1)} fusion(bf16[5,1536,768]{2,1,0:T(8,128)(2,1)} %param.6, bf16[1,128,768]{2,1,0:T(8,128)(2,1)S(1)} %rev.41), kind=kOutput, calls=%fused_computation.11 | convolution fusion | flops 301989888 | bytes 3342336 | tf_op jit(solution)/shard_map/dot_general | solution.py:61
  34.9 2.7 %rev.40 = bf16[1,128,768]{2,1,0:T(8,128)(2,1)S(1)} reverse(bf16[1,128,768]{2,1,0:T(8,128)(2,1)} %collective-permute-done.5), dimensions={2} | reverse | bytes 393216 | tf_op jit(solution)/shard_map/rev | solution.py:22
  37.5 2.6 %fusion.6 = bf16[128,1536]{1,0:T(8,128)(2,1)S(1)} fusion(f32[128,1536]{1,0:T(8,128)S(1)} %fusion.7, f32[128,1536]{1,0:T(8,128)S(1)} %fusion.1, bf16[5,1536,768]{2,1,0:T(8,128)(2,1)} %param.6, bf16[1,128,768]{2,1,0:T(8,128)(2,1)S(1)} %rev.40), kind=kOutput, calls=%fused_computation.10 | convolution fusion | flops 302579712 | bytes 4521984 | tf_op jit(solution)/shard_map/dot_general | solution.py:61
  41.3 2.7 %fusion.31 = f32[128,1536]{1,0:T(8,128)S(1)} fusion(bf16[5,1536,768]{2,1,0:T(8,128)(2,1)} %param.6, bf16[1,128,768]{2,1,0:T(8,128)(2,1)} %collective-permute-done.5), kind=kOutput, calls=%fused_computation.35 | convolution fusion | flops 301989888 | bytes 3342336 | tf_op jit(solution)/shard_map/dot_general | solution.py:61
  44.0 2.5 %fusion.9 = f32[128,1536]{1,0:T(8,128)S(1)} fusion(bf16[5,1536,768]{2,1,0:T(8,128)(2,1)} %param.6, bf16[1,128,768]{2,1,0:T(8,128)(2,1)S(1)} %copy-done.2), kind=kOutput, calls=%fused_computation.13 | convolution fusion | flops 301989888 | bytes 3342336 | tf_op jit(solution)/shard_map/dot_general | solution.py:61
  46.5 2.7 %fusion.4 = f32[128,1536]{1,0:T(8,128)S(1)} fusion(f32[128,1536]{1,0:T(8,128)S(1)} %fusion.23, f32[128,1536]{1,0:T(8,128)S(1)} %fusion.31, bf16[5,1536,768]{2,1,0:T(8,128)(2,1)} %param.6, bf16[1,128,768]{2,1,0:T(8,128)(2,1)} %collective-permute-done.4), kind=kOutput, calls=%fused_computation.8 | convolution fusion | flops 302383104 | bytes 4915200 | tf_op jit(solution)/shard_map/dot_general | solution.py:61
  49.3 3.1 %fusion.115 = (f32[1536]{0:T(1024)S(1)}, f32[128]{0:T(128)S(1)}, f32[1,128,1536]{2,1,0:T(8,128)S(1)}) fusion(bf16[1,128,1536]{2,1,0:T(8,128)(2,1)S(1)} %copy-done, f32[128]{0:T(128)S(1)} %add_rsqrt_fusion, f32[1536]{0:T(1024)S(1)} %copy-done.5, bf16[128,1536]{1,0:T(8,128)(2,1)S(1)} %reverse.7, f32[128,1536]{1,0:T(8,128)S(1)} %fusion.9, ...), kind=kOutput, calls=%fused_computation.99 | convolution fusion | flops 308083072 | bytes 5714944 | tf_op jit(solution)/shard_map/dot_general | solution.py:61
  53.7 5.5 %collective-permute-start = (bf16[1,128,1536]{2,1,0:T(8,128)(2,1)S(1)}, bf16[1,128,1536]{2,1,0:T(8,128)(2,1)S(1)}, u32[]{:S(2)}, u32[]{:S(2)}) collective-permute-start(bf16[1,128,1536]{2,1,0:T(8,128)(2,1)S(1)} %get-tuple-element.6), channel_id=1, source_target_pairs={{0,4},{1,5},{2,6},{3,7},{4,8},{5,9},{6,10},{7,11},{8,12},{9,13},{1... | collective-permute-start | bytes 1179656 | tf_op jit(solution)/shard_map/ppermute | solution.py:14
  59.2 3.6 %collective-permute-start.1 = (bf16[1,128,1536]{2,1,0:T(8,128)(2,1)S(1)}, bf16[1,128,1536]{2,1,0:T(8,128)(2,1)S(1)}, u32[]{:S(2)}, u32[]{:S(2)}) collective-permute-start(bf16[1,128,1536]{2,1,0:T(8,128)(2,1)S(1)} %get-tuple-element.6), channel_id=1, source_target_pairs={{0,2},{1,3},{2,4},{3,5},{4,6},{5,7},{6,8},{7,9},{8,10},{9,11},{10,... | collective-permute-start | bytes 1179656 | tf_op jit(solution)/shard_map/ppermute | solution.py:14
  68.8 47.5 %psum.7 = f32[1536]{0:T(1024)S(1)} all-reduce(f32[1536]{0:T(1024)S(1)} %get-tuple-element.3), channel_id=1, replica_groups=mesh['dp'=2,'ctx'=16] {'dp','ctx'}, use_global_device_ids=true, to_apply=%region_3.0 | all-reduce | flops 1536 | bytes 12288 | tf_op jit(solution)/shard_map/psum | solution.py:94
  125.9 6.7 %rev.33 = bf16[1,128,1536]{2,1,0:T(8,128)(2,1)} reverse(bf16[1,128,1536]{2,1,0:T(8,128)(2,1)} %collective-permute-done.2), dimensions={2} | reverse | bytes 786432 | tf_op jit(solution)/shard_map/rev | solution.py:22
  132.6 2.3 %fusion.33 = f32[128,768]{1,0:T(8,128)S(1)} fusion(bf16[5,1536,768]{2,1,0:T(8,128)(2,1)} %param.6, bf16[1,128,1536]{2,1,0:T(8,128)(2,1)} %rev.33), kind=kOutput, calls=%fused_computation.37 | convolution fusion | flops 301989888 | bytes 3145728 | tf_op jit(solution)/shard_map/dot_general | solution.py:51
  134.9 5.2 %rev.32 = bf16[1,128,1536]{2,1,0:T(8,128)(2,1)S(1)} reverse(bf16[1,128,1536]{2,1,0:T(8,128)(2,1)} %collective-permute-done.3), dimensions={2} | reverse | bytes 786432 | tf_op jit(solution)/shard_map/rev | solution.py:22
  142.9 2.3 %fusion.13 = f32[128,768]{1,0:T(8,128)S(1)} fusion(bf16[5,1536,768]{2,1,0:T(8,128)(2,1)} %param.6, bf16[1,128,1536]{2,1,0:T(8,128)(2,1)} %collective-permute-done.3), kind=kOutput, calls=%fused_computation.17 | convolution fusion | flops 301989888 | bytes 3145728 | tf_op jit(solution)/shard_map/dot_general | solution.py:51
  145.2 2.3 %fusion.19 = f32[128,768]{1,0:T(8,128)S(1)} fusion(bf16[5,1536,768]{2,1,0:T(8,128)(2,1)} %param.6, bf16[1,128,1536]{2,1,0:T(8,128)(2,1)} %collective-permute-done.2), kind=kOutput, calls=%fused_computation.23 | convolution fusion | flops 301989888 | bytes 3145728 | tf_op jit(solution)/shard_map/dot_general | solution.py:51
  149.6 2.9 %fusion.96 = bf16[1,128,768]{2,1,0:T(8,128)(2,1)} fusion(f32[128,768]{1,0:T(8,128)S(1)} %fusion.13, f32[128,768]{1,0:T(8,128)S(1)} %fusion.19, f32[128,768]{1,0:T(8,128)S(1)} %fusion.27, f32[128,768]{1,0:T(8,128)S(1)} %fusion.35, bf16[5,1536,768]{2,1,0:T(8,128)(2,1)} %param.6, bf16[1,128,1536]{2,1,0:T(8,128)(2,1)S(1)} %collective-permute-done, ...), kind=kOutput, calls=%fused_computation.78 | convolution fusion | flops 302678016 | bytes 4718592 | tf_op jit(solution)/shard_map/dot_general | solution.py:51
  (42 shorter events, 30.1 us)
Async XLA Ops:
  0.6 20.1 %collective-permute-start.6 = (bf16[1,128,768]{2,1,0:T(8,128)(2,1)}, bf16[1,128,768]{2,1,0:T(8,128)(2,1)S(1)}, u32[]{:S(2)}, u32[]{:S(2)}) collective-permute-start(bf16[1,128,768]{2,1,0:T(8,128)(2,1)} %param.7), channel_id=1, source_target_pairs={{0,2},{1,3},{2,4},{3,5},{4,6},{5,7},{6,8},{7,9},{8,10},{9,11},{10,... | collective-permute-start | bytes 589832 | tf_op jit(solution)/shard_map/ppermute | solution.py:14
  5.5 18.4 %collective-permute-start.7 = (bf16[1,128,768]{2,1,0:T(8,128)(2,1)}, bf16[1,128,768]{2,1,0:T(8,128)(2,1)S(1)}, u32[]{:S(2)}, u32[]{:S(2)}) collective-permute-start(bf16[1,128,768]{2,1,0:T(8,128)(2,1)} %param.7), channel_id=1, source_target_pairs={{0,4},{1,5},{2,6},{3,7},{4,8},{5,9},{6,10},{7,11},{8,12},{9,13},{1... | collective-permute-start | bytes 589832 | tf_op jit(solution)/shard_map/ppermute | solution.py:14
  9.0 20.5 %collective-permute-start.4 = (bf16[1,128,768]{2,1,0:T(8,128)(2,1)}, bf16[1,128,768]{2,1,0:T(8,128)(2,1)}, u32[]{:S(2)}, u32[]{:S(2)}) collective-permute-start(bf16[1,128,768]{2,1,0:T(8,128)(2,1)} %param.7), channel_id=1, source_target_pairs={{4,0},{5,1},{6,2},{7,3},{8,4},{9,5},{10,6},{11,7},{12,8},{13,9},{1... | collective-permute-start | bytes 589832 | tf_op jit(solution)/shard_map/ppermute | solution.py:14
  10.3 24.5 %collective-permute-start.5 = (bf16[1,128,768]{2,1,0:T(8,128)(2,1)}, bf16[1,128,768]{2,1,0:T(8,128)(2,1)}, u32[]{:S(2)}, u32[]{:S(2)}) collective-permute-start(bf16[1,128,768]{2,1,0:T(8,128)(2,1)} %param.7), channel_id=1, source_target_pairs={{2,0},{3,1},{4,2},{5,3},{6,4},{7,5},{8,6},{9,7},{10,8},{11,9},{12,... | collective-permute-start | bytes 589832 | tf_op jit(solution)/shard_map/ppermute | solution.py:14
  20.7 3.2 %copy-start.3 = (bf16[1,128,768]{2,1,0:T(8,128)(2,1)}, bf16[1,128,768]{2,1,0:T(8,128)(2,1)S(1)}, u32[]{:S(2)}) copy-start(bf16[1,128,768]{2,1,0:T(8,128)(2,1)S(1)} %collective-permute-done.6) | copy-start | bytes 589828
  23.9 0.7 copy-start.1
  26.8 22.4 %copy-start = (bf16[1,128,1536]{2,1,0:T(8,128)(2,1)S(1)}, bf16[1,128,1536]{2,1,0:T(8,128)(2,1)}, u32[]{:S(2)}) copy-start(bf16[1,128,1536]{2,1,0:T(8,128)(2,1)} %param.4) | copy-start | bytes 1179652
  26.8 22.4 %copy-start.5 = (f32[1536]{0:T(1024)S(1)}, f32[1536]{0:T(1024)}, u32[]{:S(2)}) copy-start(f32[1536]{0:T(1024)} %param.5) | copy-start | bytes 18436
  29.6 14.4 %copy-start.2 = (bf16[1,128,768]{2,1,0:T(8,128)(2,1)S(1)}, bf16[1,128,768]{2,1,0:T(8,128)(2,1)}, u32[]{:S(2)}) copy-start(bf16[1,128,768]{2,1,0:T(8,128)(2,1)} %copy-done.1) | copy-start | bytes 589828
  40.1 9.2 %copy-start.4 = (bf16[1,128,768]{2,1,0:T(8,128)(2,1)S(1)}, bf16[1,128,768]{2,1,0:T(8,128)(2,1)}, u32[]{:S(2)}) copy-start(bf16[1,128,768]{2,1,0:T(8,128)(2,1)} %copy-done.3) | copy-start | bytes 589828
  53.7 65.4 %collective-permute-start = (bf16[1,128,1536]{2,1,0:T(8,128)(2,1)S(1)}, bf16[1,128,1536]{2,1,0:T(8,128)(2,1)S(1)}, u32[]{:S(2)}, u32[]{:S(2)}) collective-permute-start(bf16[1,128,1536]{2,1,0:T(8,128)(2,1)S(1)} %get-tuple-element.6), channel_id=1, source_target_pairs={{0,4},{1,5},{2,6},{3,7},{4,8},{5,9},{6,10},{7,11},{8,12},{9,13},{1... | collective-permute-start | bytes 1179656 | tf_op jit(solution)/shard_map/ppermute | solution.py:14
  59.2 63.3 %collective-permute-start.1 = (bf16[1,128,1536]{2,1,0:T(8,128)(2,1)S(1)}, bf16[1,128,1536]{2,1,0:T(8,128)(2,1)S(1)}, u32[]{:S(2)}, u32[]{:S(2)}) collective-permute-start(bf16[1,128,1536]{2,1,0:T(8,128)(2,1)S(1)} %get-tuple-element.6), channel_id=1, source_target_pairs={{0,2},{1,3},{2,4},{3,5},{4,6},{5,7},{6,8},{7,9},{8,10},{9,11},{10,... | collective-permute-start | bytes 1179656 | tf_op jit(solution)/shard_map/ppermute | solution.py:14
  62.8 63.0 %collective-permute-start.2 = (bf16[1,128,1536]{2,1,0:T(8,128)(2,1)S(1)}, bf16[1,128,1536]{2,1,0:T(8,128)(2,1)}, u32[]{:S(2)}, u32[]{:S(2)}) collective-permute-start(bf16[1,128,1536]{2,1,0:T(8,128)(2,1)S(1)} %get-tuple-element.6), channel_id=1, source_target_pairs={{2,0},{3,1},{4,2},{5,3},{6,4},{7,5},{8,6},{9,7},{10,8},{11,9},{12,... | collective-permute-start | bytes 1179656 | tf_op jit(solution)/shard_map/ppermute | solution.py:14
  64.1 70.7 %collective-permute-start.3 = (bf16[1,128,1536]{2,1,0:T(8,128)(2,1)S(1)}, bf16[1,128,1536]{2,1,0:T(8,128)(2,1)}, u32[]{:S(2)}, u32[]{:S(2)}) collective-permute-start(bf16[1,128,1536]{2,1,0:T(8,128)(2,1)S(1)} %get-tuple-element.6), channel_id=1, source_target_pairs={{4,0},{5,1},{6,2},{7,3},{8,4},{9,5},{10,6},{11,7},{12,8},{13,9},{1... | collective-permute-start | bytes 1179656 | tf_op jit(solution)/shard_map/ppermute | solution.py:14
where the time goes:
time: 155 us; the launch traced here: 153 us
  matrix products  49.2 us (32%)
  blocking collectives  47.5 us (31%)
  local copies, waits for them, and re-layouts  28.9 us (19%)
  starting transfers between devices  22.7 us (15%)
  other arithmetic  3.03 us (2%)
    psum x1, blocking collectives, per_device(): summed = lax.psum(partial_sum, ('dp', 'ctx'))  47.5 us
    dot_general x10, matrix products, apply_backward(): lax.dot_general(flat_rows, weight[tap_index], (((1,), (1,)), ((), ())), p...  26.6 us
    rev x10, local copies, waits for them, and re-layouts, flip_channels(): return values[:, :, ::-1]  26.4 us
    ppermute x8, starting transfers between devices, shifted(): return lax.ppermute(block, axis, route)  22.7 us
    dot_general x10, matrix products, apply_forward(): jnp.dot(flat_rows, weight[tap_index], preferred_element_type=jnp.float32)  22.6 us
  transfers between devices with their start and end apart: 8, of which 0 were waited for; matrix products, arithmetic and copies ran while one was open for 29% of the time, Pallas kernels for 0%

commit v1 on v0

--- a/solution.py
+++ b/solution.py
@@ -91,7 +91,7 @@
     _, pullback = jax.vjp(activate, scaled)
     grad_scaled = pullback(grad_hidden)[0]
     partial_sum = jnp.sum(grad_scaled * normed, axis=(0, 1))
-    summed = lax.psum(partial_sum, ("dp", "ctx"))
+    summed = lax.psum(lax.psum(partial_sum, "ctx"), "dp")
     total_rows = features.shape[0] * features.shape[1] * lax.axis_size("dp") * lax.axis_size("ctx")
     gain_grad = summed / math.sqrt(total_rows)
     grad_normed = grad_scaled * gain

time: 155 us -> 149 us (0.961)
  blocking collectives: 47.5 us -> 40.9 us
    psum x1 -> x2, blocking collectives: 47.5 us -> 40.9 us  [per_device(): summed = lax.psum(lax.psum(partial_sum, 'ctx'), 'dp')]
  transfers between devices with their start and end apart: 8 -> 8, of which waited for: 0 -> 0; matrix products, arithmetic and copies ran while one was open for 29% -> 30% of each run, Pallas kernels for 0% -> 0%
where the time goes in v1:
time: 149 us; the launch traced here: 146 us
  matrix products  49.2 us (33%)
  blocking collectives  40.9 us (27%)
  local copies, waits for them, and re-layouts  28.9 us (19%)
  starting transfers between devices  22.7 us (15%)
  other arithmetic  3.03 us (2%)
    psum x2, blocking collectives, per_device(): summed = lax.psum(lax.psum(partial_sum, 'ctx'), 'dp')  40.9 us
    dot_general x10, matrix products, apply_backward(): lax.dot_general(flat_rows, weight[tap_index], (((1,), (1,)), ((), ())), p...  26.6 us
    rev x10, local copies, waits for them, and re-layouts, flip_channels(): return values[:, :, ::-1]  26.4 us
    ppermute x8, starting transfers between devices, shifted(): return lax.ppermute(block, axis, route)  22.7 us
    dot_general x10, matrix products, apply_forward(): jnp.dot(flat_rows, weight[tap_index], preferred_element_type=jnp.float32)  22.6 us
  transfers between devices with their start and end apart: 8, of which 0 were waited for; matrix products, arithmetic and copies ran while one was open for 30% of the time, Pallas kernels for 0%

profile of v1, /device:TPU:0, one launch (start us, length us, event | category | flops | bytes accessed | tf_op | source)
XLA Modules:
  0.0 145.9 jit_solution(11541098812302060212)
XLA Ops:
  0.6 4.9 %collective-permute-start.6 = (bf16[1,128,768]{2,1,0:T(8,128)(2,1)}, bf16[1,128,768]{2,1,0:T(8,128)(2,1)S(1)}, u32[]{:S(2)}, u32[]{:S(2)}) collective-permute-start(bf16[1,128,768]{2,1,0:T(8,128)(2,1)} %param.7), channel_id=1, source_target_pairs={{0,2},{1,3},{2,4},{3,5},{4,6},{5,7},{6,8},{7,9},{8,10},{9,11},{10,... | collective-permute-start | bytes 589832 | tf_op jit(solution)/shard_map/ppermute | solution.py:14
  5.5 3.5 %collective-permute-start.7 = (bf16[1,128,768]{2,1,0:T(8,128)(2,1)}, bf16[1,128,768]{2,1,0:T(8,128)(2,1)S(1)}, u32[]{:S(2)}, u32[]{:S(2)}) collective-permute-start(bf16[1,128,768]{2,1,0:T(8,128)(2,1)} %param.7), channel_id=1, source_target_pairs={{0,4},{1,5},{2,6},{3,7},{4,8},{5,9},{6,10},{7,11},{8,12},{9,13},{1... | collective-permute-start | bytes 589832 | tf_op jit(solution)/shard_map/ppermute | solution.py:14
  11.6 2.7 %rev.39 = bf16[1,128,768]{2,1,0:T(8,128)(2,1)S(1)} reverse(bf16[1,128,768]{2,1,0:T(8,128)(2,1)} %param.7), dimensions={2} | reverse | bytes 393216 | tf_op jit(solution)/shard_map/rev | solution.py:22
  14.3 2.7 %fusion.23 = f32[128,1536]{1,0:T(8,128)S(1)} fusion(bf16[5,1536,768]{2,1,0:T(8,128)(2,1)} %param.6, bf16[1,128,768]{2,1,0:T(8,128)(2,1)} %param.7), kind=kOutput, calls=%fused_computation.27 | convolution fusion | flops 301989888 | bytes 3342336 | tf_op jit(solution)/shard_map/dot_general | solution.py:61
  17.0 2.6 %fusion.21 = f32[128,1536]{1,0:T(8,128)S(1)} fusion(bf16[5,1536,768]{2,1,0:T(8,128)(2,1)} %param.6, bf16[1,128,768]{2,1,0:T(8,128)(2,1)S(1)} %rev.39), kind=kOutput, calls=%fused_computation.25 | convolution fusion | flops 301989888 | bytes 3342336 | tf_op jit(solution)/shard_map/dot_general | solution.py:61
  21.4 2.5 %fusion.29 = f32[128,1536]{1,0:T(8,128)S(1)} fusion(bf16[5,1536,768]{2,1,0:T(8,128)(2,1)} %param.6, bf16[1,128,768]{2,1,0:T(8,128)(2,1)S(1)} %rev.38), kind=kOutput, calls=%fused_computation.33 | convolution fusion | flops 301989888 | bytes 3342336 | tf_op jit(solution)/shard_map/dot_general | solution.py:61
  26.8 2.7 %fusion.1 = f32[128,1536]{1,0:T(8,128)S(1)} fusion(f32[128,1536]{1,0:T(8,128)S(1)} %fusion.21, f32[128,1536]{1,0:T(8,128)S(1)} %fusion.29, bf16[5,1536,768]{2,1,0:T(8,128)(2,1)} %param.6, bf16[1,128,768]{2,1,0:T(8,128)(2,1)} %rev.37), kind=kOutput, calls=%fused_computation.3 | convolution fusion | flops 302383104 | bytes 4915200 | tf_op jit(solution)/shard_map/dot_general | solution.py:61
  29.6 2.7 %rev.41 = bf16[1,128,768]{2,1,0:T(8,128)(2,1)S(1)} reverse(bf16[1,128,768]{2,1,0:T(8,128)(2,1)} %collective-permute-done.4), dimensions={2} | reverse | bytes 393216 | tf_op jit(solution)/shard_map/rev | solution.py:22
  32.3 2.6 %fusion.7 = f32[128,1536]{1,0:T(8,128)S(1)} fusion(bf16[5,1536,768]{2,1,0:T(8,128)(2,1)} %param.6, bf16[1,128,768]{2,1,0:T(8,128)(2,1)S(1)} %rev.41), kind=kOutput, calls=%fused_computation.11 | convolution fusion | flops 301989888 | bytes 3342336 | tf_op jit(solution)/shard_map/dot_general | solution.py:61
  34.9 2.7 %rev.40 = bf16[1,128,768]{2,1,0:T(8,128)(2,1)S(1)} reverse(bf16[1,128,768]{2,1,0:T(8,128)(2,1)} %collective-permute-done.5), dimensions={2} | reverse | bytes 393216 | tf_op jit(solution)/shard_map/rev | solution.py:22
  37.5 2.6 %fusion.6 = bf16[128,1536]{1,0:T(8,128)(2,1)S(1)} fusion(f32[128,1536]{1,0:T(8,128)S(1)} %fusion.7, f32[128,1536]{1,0:T(8,128)S(1)} %fusion.1, bf16[5,1536,768]{2,1,0:T(8,128)(2,1)} %param.6, bf16[1,128,768]{2,1,0:T(8,128)(2,1)S(1)} %rev.40), kind=kOutput, calls=%fused_computation.10 | convolution fusion | flops 302579712 | bytes 4521984 | tf_op jit(solution)/shard_map/dot_general | solution.py:61
  41.3 2.7 %fusion.31 = f32[128,1536]{1,0:T(8,128)S(1)} fusion(bf16[5,1536,768]{2,1,0:T(8,128)(2,1)} %param.6, bf16[1,128,768]{2,1,0:T(8,128)(2,1)} %collective-permute-done.5), kind=kOutput, calls=%fused_computation.35 | convolution fusion | flops 301989888 | bytes 3342336 | tf_op jit(solution)/shard_map/dot_general | solution.py:61
  44.0 2.5 %fusion.9 = f32[128,1536]{1,0:T(8,128)S(1)} fusion(bf16[5,1536,768]{2,1,0:T(8,128)(2,1)} %param.6, bf16[1,128,768]{2,1,0:T(8,128)(2,1)S(1)} %copy-done.2), kind=kOutput, calls=%fused_computation.13 | convolution fusion | flops 301989888 | bytes 3342336 | tf_op jit(solution)/shard_map/dot_general | solution.py:61
  46.5 2.7 %fusion.4 = f32[128,1536]{1,0:T(8,128)S(1)} fusion(f32[128,1536]{1,0:T(8,128)S(1)} %fusion.23, f32[128,1536]{1,0:T(8,128)S(1)} %fusion.31, bf16[5,1536,768]{2,1,0:T(8,128)(2,1)} %param.6, bf16[1,128,768]{2,1,0:T(8,128)(2,1)} %collective-permute-done.4), kind=kOutput, calls=%fused_computation.8 | convolution fusion | flops 302383104 | bytes 4915200 | tf_op jit(solution)/shard_map/dot_general | solution.py:61
  49.3 3.1 %fusion.115 = (f32[1536]{0:T(1024)S(1)}, f32[128]{0:T(128)S(1)}, f32[1,128,1536]{2,1,0:T(8,128)S(1)}) fusion(bf16[1,128,1536]{2,1,0:T(8,128)(2,1)S(1)} %copy-done, f32[128]{0:T(128)S(1)} %add_rsqrt_fusion, f32[1536]{0:T(1024)S(1)} %copy-done.5, bf16[128,1536]{1,0:T(8,128)(2,1)S(1)} %reverse.7, f32[128,1536]{1,0:T(8,128)S(1)} %fusion.9, ...), kind=kOutput, calls=%fused_computation.99 | convolution fusion | flops 308083072 | bytes 5714944 | tf_op jit(solution)/shard_map/dot_general | solution.py:61
  53.7 5.5 %collective-permute-start = (bf16[1,128,1536]{2,1,0:T(8,128)(2,1)S(1)}, bf16[1,128,1536]{2,1,0:T(8,128)(2,1)S(1)}, u32[]{:S(2)}, u32[]{:S(2)}) collective-permute-start(bf16[1,128,1536]{2,1,0:T(8,128)(2,1)S(1)} %get-tuple-element.6), channel_id=1, source_target_pairs={{0,4},{1,5},{2,6},{3,7},{4,8},{5,9},{6,10},{7,11},{8,12},{9,13},{1... | collective-permute-start | bytes 1179656 | tf_op jit(solution)/shard_map/ppermute | solution.py:14
  59.2 3.6 %collective-permute-start.1 = (bf16[1,128,1536]{2,1,0:T(8,128)(2,1)S(1)}, bf16[1,128,1536]{2,1,0:T(8,128)(2,1)S(1)}, u32[]{:S(2)}, u32[]{:S(2)}) collective-permute-start(bf16[1,128,1536]{2,1,0:T(8,128)(2,1)S(1)} %get-tuple-element.6), channel_id=1, source_target_pairs={{0,2},{1,3},{2,4},{3,5},{4,6},{5,7},{6,8},{7,9},{8,10},{9,11},{10,... | collective-permute-start | bytes 1179656 | tf_op jit(solution)/shard_map/ppermute | solution.py:14
  68.8 35.9 %psum.14 = f32[1536]{0:T(1024)S(1)} all-reduce(f32[1536]{0:T(1024)S(1)} %get-tuple-element.3), channel_id=1, replica_groups=mesh['dp'=2,'ctx'=16] {'ctx'}, use_global_device_ids=true, to_apply=%region_3.0 | all-reduce | flops 1536 | bytes 12288 | tf_op jit(solution)/shard_map/psum | solution.py:94
  104.7 5.0 %psum.15 = f32[1536]{0:T(1024)S(1)} all-reduce(f32[1536]{0:T(1024)S(1)} %psum.14), channel_id=1, replica_groups=mesh['dp'=2,'ctx'=16] {'dp'}, use_global_device_ids=true, to_apply=%region_4.0 | all-reduce | flops 1536 | bytes 12288 | tf_op jit(solution)/shard_map/psum | solution.py:94
  119.2 6.7 %rev.33 = bf16[1,128,1536]{2,1,0:T(8,128)(2,1)} reverse(bf16[1,128,1536]{2,1,0:T(8,128)(2,1)} %collective-permute-done.2), dimensions={2} | reverse | bytes 786432 | tf_op jit(solution)/shard_map/rev | solution.py:22
  128.2 5.2 %rev.32 = bf16[1,128,1536]{2,1,0:T(8,128)(2,1)S(1)} reverse(bf16[1,128,1536]{2,1,0:T(8,128)(2,1)} %collective-permute-done.3), dimensions={2} | reverse | bytes 786432 | tf_op jit(solution)/shard_map/rev | solution.py:22
  136.2 2.3 %fusion.13 = f32[128,768]{1,0:T(8,128)S(1)} fusion(bf16[5,1536,768]{2,1,0:T(8,128)(2,1)} %param.6, bf16[1,128,1536]{2,1,0:T(8,128)(2,1)} %collective-permute-done.3), kind=kOutput, calls=%fused_computation.17 | convolution fusion | flops 301989888 | bytes 3145728 | tf_op jit(solution)/shard_map/dot_general | solution.py:51
  138.5 2.3 %fusion.19 = f32[128,768]{1,0:T(8,128)S(1)} fusion(bf16[5,1536,768]{2,1,0:T(8,128)(2,1)} %param.6, bf16[1,128,1536]{2,1,0:T(8,128)(2,1)} %collective-permute-done.2), kind=kOutput, calls=%fused_computation.23 | convolution fusion | flops 301989888 | bytes 3145728 | tf_op jit(solution)/shard_map/dot_general | solution.py:51
  143.0 2.9 %fusion.96 = bf16[1,128,768]{2,1,0:T(8,128)(2,1)} fusion(f32[128,768]{1,0:T(8,128)S(1)} %fusion.13, f32[128,768]{1,0:T(8,128)S(1)} %fusion.19, f32[128,768]{1,0:T(8,128)S(1)} %fusion.27, f32[128,768]{1,0:T(8,128)S(1)} %fusion.35, bf16[5,1536,768]{2,1,0:T(8,128)(2,1)} %param.6, bf16[1,128,1536]{2,1,0:T(8,128)(2,1)S(1)} %collective-permute-done, ...), kind=kOutput, calls=%fused_computation.78 | convolution fusion | flops 302678016 | bytes 4718592 | tf_op jit(solution)/shard_map/dot_general | solution.py:51
  (43 shorter events, 32.4 us)
Async XLA Ops:
  0.6 20.1 %collective-permute-start.6 = (bf16[1,128,768]{2,1,0:T(8,128)(2,1)}, bf16[1,128,768]{2,1,0:T(8,128)(2,1)S(1)}, u32[]{:S(2)}, u32[]{:S(2)}) collective-permute-start(bf16[1,128,768]{2,1,0:T(8,128)(2,1)} %param.7), channel_id=1, source_target_pairs={{0,2},{1,3},{2,4},{3,5},{4,6},{5,7},{6,8},{7,9},{8,10},{9,11},{10,... | collective-permute-start | bytes 589832 | tf_op jit(solution)/shard_map/ppermute | solution.py:14
  5.5 18.4 %collective-permute-start.7 = (bf16[1,128,768]{2,1,0:T(8,128)(2,1)}, bf16[1,128,768]{2,1,0:T(8,128)(2,1)S(1)}, u32[]{:S(2)}, u32[]{:S(2)}) collective-permute-start(bf16[1,128,768]{2,1,0:T(8,128)(2,1)} %param.7), channel_id=1, source_target_pairs={{0,4},{1,5},{2,6},{3,7},{4,8},{5,9},{6,10},{7,11},{8,12},{9,13},{1... | collective-permute-start | bytes 589832 | tf_op jit(solution)/shard_map/ppermute | solution.py:14
  9.0 20.5 %collective-permute-start.4 = (bf16[1,128,768]{2,1,0:T(8,128)(2,1)}, bf16[1,128,768]{2,1,0:T(8,128)(2,1)}, u32[]{:S(2)}, u32[]{:S(2)}) collective-permute-start(bf16[1,128,768]{2,1,0:T(8,128)(2,1)} %param.7), channel_id=1, source_target_pairs={{4,0},{5,1},{6,2},{7,3},{8,4},{9,5},{10,6},{11,7},{12,8},{13,9},{1... | collective-permute-start | bytes 589832 | tf_op jit(solution)/shard_map/ppermute | solution.py:14
  10.3 24.5 %collective-permute-start.5 = (bf16[1,128,768]{2,1,0:T(8,128)(2,1)}, bf16[1,128,768]{2,1,0:T(8,128)(2,1)}, u32[]{:S(2)}, u32[]{:S(2)}) collective-permute-start(bf16[1,128,768]{2,1,0:T(8,128)(2,1)} %param.7), channel_id=1, source_target_pairs={{2,0},{3,1},{4,2},{5,3},{6,4},{7,5},{8,6},{9,7},{10,8},{11,9},{12,... | collective-permute-start | bytes 589832 | tf_op jit(solution)/shard_map/ppermute | solution.py:14
  20.7 3.2 %copy-start.3 = (bf16[1,128,768]{2,1,0:T(8,128)(2,1)}, bf16[1,128,768]{2,1,0:T(8,128)(2,1)S(1)}, u32[]{:S(2)}) copy-start(bf16[1,128,768]{2,1,0:T(8,128)(2,1)S(1)} %collective-permute-done.6) | copy-start | bytes 589828
  23.9 0.7 copy-start.1
  26.8 22.4 %copy-start = (bf16[1,128,1536]{2,1,0:T(8,128)(2,1)S(1)}, bf16[1,128,1536]{2,1,0:T(8,128)(2,1)}, u32[]{:S(2)}) copy-start(bf16[1,128,1536]{2,1,0:T(8,128)(2,1)} %param.4) | copy-start | bytes 1179652
  26.8 22.4 %copy-start.5 = (f32[1536]{0:T(1024)S(1)}, f32[1536]{0:T(1024)}, u32[]{:S(2)}) copy-start(f32[1536]{0:T(1024)} %param.5) | copy-start | bytes 18436
  29.6 14.4 %copy-start.2 = (bf16[1,128,768]{2,1,0:T(8,128)(2,1)S(1)}, bf16[1,128,768]{2,1,0:T(8,128)(2,1)}, u32[]{:S(2)}) copy-start(bf16[1,128,768]{2,1,0:T(8,128)(2,1)} %copy-done.1) | copy-start | bytes 589828
  40.1 9.2 %copy-start.4 = (bf16[1,128,768]{2,1,0:T(8,128)(2,1)S(1)}, bf16[1,128,768]{2,1,0:T(8,128)(2,1)}, u32[]{:S(2)}) copy-start(bf16[1,128,768]{2,1,0:T(8,128)(2,1)} %copy-done.3) | copy-start | bytes 589828
  53.7 58.8 %collective-permute-start = (bf16[1,128,1536]{2,1,0:T(8,128)(2,1)S(1)}, bf16[1,128,1536]{2,1,0:T(8,128)(2,1)S(1)}, u32[]{:S(2)}, u32[]{:S(2)}) collective-permute-start(bf16[1,128,1536]{2,1,0:T(8,128)(2,1)S(1)} %get-tuple-element.6), channel_id=1, source_target_pairs={{0,4},{1,5},{2,6},{3,7},{4,8},{5,9},{6,10},{7,11},{8,12},{9,13},{1... | collective-permute-start | bytes 1179656 | tf_op jit(solution)/shard_map/ppermute | solution.py:14
  59.2 56.6 %collective-permute-start.1 = (bf16[1,128,1536]{2,1,0:T(8,128)(2,1)S(1)}, bf16[1,128,1536]{2,1,0:T(8,128)(2,1)S(1)}, u32[]{:S(2)}, u32[]{:S(2)}) collective-permute-start(bf16[1,128,1536]{2,1,0:T(8,128)(2,1)S(1)} %get-tuple-element.6), channel_id=1, source_target_pairs={{0,2},{1,3},{2,4},{3,5},{4,6},{5,7},{6,8},{7,9},{8,10},{9,11},{10,... | collective-permute-start | bytes 1179656 | tf_op jit(solution)/shard_map/ppermute | solution.py:14
  62.8 56.4 %collective-permute-start.2 = (bf16[1,128,1536]{2,1,0:T(8,128)(2,1)S(1)}, bf16[1,128,1536]{2,1,0:T(8,128)(2,1)}, u32[]{:S(2)}, u32[]{:S(2)}) collective-permute-start(bf16[1,128,1536]{2,1,0:T(8,128)(2,1)S(1)} %get-tuple-element.6), channel_id=1, source_target_pairs={{2,0},{3,1},{4,2},{5,3},{6,4},{7,5},{8,6},{9,7},{10,8},{11,9},{12,... | collective-permute-start | bytes 1179656 | tf_op jit(solution)/shard_map/ppermute | solution.py:14
  64.1 64.1 %collective-permute-start.3 = (bf16[1,128,1536]{2,1,0:T(8,128)(2,1)S(1)}, bf16[1,128,1536]{2,1,0:T(8,128)(2,1)}, u32[]{:S(2)}, u32[]{:S(2)}) collective-permute-start(bf16[1,128,1536]{2,1,0:T(8,128)(2,1)S(1)} %get-tuple-element.6), channel_id=1, source_target_pairs={{4,0},{5,1},{6,2},{7,3},{8,4},{9,5},{10,6},{11,7},{12,8},{13,9},{1... | collective-permute-start | bytes 1179656 | tf_op jit(solution)/shard_map/ppermute | solution.py:14
